TPU v7x, 32 devices: a whole 2x2x4 slice. The times are simulated.
32 devices in a mesh: dp: 8 (over y, x, core), expert: 4 (over z).
Axes of the slice: x: 2, y: 2, z: 4, core: 2. Of those that a mesh axis runs over, the one named last changes fastest.
Arguments:
- tokens: bfloat16 [512, 6144], P('dp', 'expert'), may hold values from -6 to 6
- cotangent: bfloat16 [512, 6144], P('dp', 'expert'), may hold values from -6 to 6
- expert_ids: int32 [512, 2], P('dp'), may hold values from 0 to 7, all different within a row; in each aligned block of 64 rows (0 to 63, 64 to 127, ...) at most 48 rows name the same one
- routing_weights: bfloat16 [512, 2], P('dp'), may hold values from 0.099609375 to 0.8984375
- w_gate: bfloat16 [6144, 65536], P(None, ('dp', 'expert')), may hold values from -0.078125 to 0.078125
- w_up: bfloat16 [6144, 65536], P(None, ('dp', 'expert')), may hold values from -0.078125 to 0.078125
- w_down: bfloat16 [65536, 6144], P(('dp', 'expert')), may hold values from -0.0625 to 0.0625
- embedding: bfloat16 [32768, 6144], P(('dp', 'expert')), may hold values from -0.078125 to 0.078125
Outputs:
- input_grad: bfloat16 [512, 6144], P('dp', 'expert')
- scores: float32 [512, 32768], P(None, ('dp', 'expert'))
Inputs may be any that keep to these rules, and one draw needn't show every extreme that they name: `expert_ids`: the 2 ids of a token differ. Within the 64 rows of one index of dp no expert is named more than 48 times, a bound that some block reaches.
All inputs are finite; a program needn't handle non-finite values.
Results may differ from a plain program's by a relative error of at most 0.012.
Values may be sent and summed in bfloat16 or wider, within the bound.
A program may use at most 256 MiB of HBM per device.

v0:
```python
import jax
import jax.numpy as jnp
from jax import lax
from jax.sharding import PartitionSpec as P

E = 8
TOP = 2
MOST = 48


def owner_work(rows_x, rows_dy, gates, w_gate, w_up, w_down):
    sources, slots, width = rows_x.shape
    flat_x = rows_x.reshape(sources * slots, width)
    flat_dy = rows_dy.reshape(sources * slots, width)
    contract = (((1,), (1,)), ((), ()))
    gate_pre = jnp.dot(flat_x, w_gate, preferred_element_type=jnp.float32)
    up_pre = jnp.dot(flat_x, w_up, preferred_element_type=jnp.float32)
    down_back = lax.dot_general(flat_dy, w_down, contract, preferred_element_type=jnp.float32)
    scaled = gates.reshape(sources * slots, 1).astype(jnp.float32) * down_back
    sigma = jax.nn.sigmoid(gate_pre)
    grad_gate = (scaled * up_pre * sigma * (1.0 + gate_pre * (1.0 - sigma))).astype(jnp.bfloat16)
    grad_up = (scaled * gate_pre * sigma).astype(jnp.bfloat16)
    partial_rows = lax.dot_general(grad_gate, w_gate, contract, preferred_element_type=jnp.float32)
    partial_rows = partial_rows + lax.dot_general(
        grad_up, w_up, contract, preferred_element_type=jnp.float32
    )
    return partial_rows.reshape(sources, slots, width)


def on_device(tokens, cotangent, expert_ids, routing_weights, w_gate, w_up, w_down, embedding):
    dp_count = lax.axis_size("dp")
    owners = dp_count // E
    tok_rows = tokens.shape[0]
    pair_count = tok_rows * TOP
    flat_ids = expert_ids.reshape(pair_count)
    expert_iota = jnp.arange(E, dtype=jnp.int32)
    onehot = (flat_ids[:, None] == expert_iota[None, :]).astype(jnp.float32)
    pair_iota = jnp.arange(pair_count, dtype=jnp.int32)
    earlier = (pair_iota[:, None] > pair_iota[None, :]).astype(jnp.float32)
    before = jnp.dot(earlier, onehot, precision=lax.Precision.HIGHEST)
    slot_rank = jnp.sum(before * onehot, axis=1).astype(jnp.int32)
    slot_of = flat_ids * MOST + slot_rank
    slot_iota = jnp.arange(E * MOST, dtype=jnp.int32)
    placed = slot_iota[:, None] == slot_of[None, :]
    flat_weights = routing_weights.reshape(pair_count).astype(jnp.float32)
    gate_slots = jnp.sum(jnp.where(placed, flat_weights[None, :], 0.0), axis=1).astype(jnp.bfloat16)
    select_rows = jnp.sum(
        placed.reshape(E * MOST, tok_rows, TOP).astype(jnp.float32), axis=2
    ).astype(jnp.bfloat16)
    send_gates = jnp.repeat(gate_slots.reshape(E, MOST), owners, axis=0)

    def dispatch(rows):
        packed = jnp.dot(select_rows, rows, preferred_element_type=jnp.float32).astype(jnp.bfloat16)
        return jnp.repeat(packed.reshape(E, MOST, rows.shape[1]), owners, axis=0)

    whole_x, whole_dy = (
        lax.all_gather(tokens, "expert", axis=1, tiled=True),
        lax.all_gather(cotangent, "expert", axis=1, tiled=True),
    )
    recv_x, recv_dy, recv_gates = (
        lax.all_to_all(dispatch(whole_x), "dp", split_axis=0, concat_axis=0, tiled=True),
        lax.all_to_all(dispatch(whole_dy), "dp", split_axis=0, concat_axis=0, tiled=True),
        lax.all_to_all(send_gates, "dp", split_axis=0, concat_axis=0, tiled=True),
    )
    partial_rows = owner_work(recv_x, recv_dy, recv_gates, w_gate, w_up, w_down).astype(
        jnp.bfloat16
    )
    came_back = lax.all_to_all(partial_rows, "dp", split_axis=0, concat_axis=0, tiled=True)
    returned = lax.psum_scatter(
        came_back.astype(jnp.float32).astype(jnp.bfloat16),
        "expert",
        scatter_dimension=2,
        tiled=True,
    )
    spread = jnp.repeat(select_rows.reshape(E, MOST, tok_rows), owners, axis=0).reshape(
        dp_count * MOST, tok_rows
    )
    feature_count = returned.shape[2]
    input_grad = lax.dot_general(
        spread,
        returned.reshape(dp_count * MOST, feature_count),
        (((0,), (0,)), ((), ())),
        preferred_element_type=jnp.float32,
    ).astype(jnp.bfloat16)
    whole_grad = lax.all_gather(input_grad, "expert", axis=1, tiled=True)
    scores = -lax.dot_general(
        lax.all_gather(whole_grad, "dp", axis=0, tiled=True),
        embedding,
        (((1,), (1,)), ((), ())),
        preferred_element_type=jnp.float32,
    )
    return (input_grad, scores)


def solution(mesh):
    placed = (
        P("dp", "expert"),
        P("dp", "expert"),
        P("dp", None),
        P("dp", None),
        P(None, ("dp", "expert")),
        P(None, ("dp", "expert")),
        P(("dp", "expert"), None),
        P(("dp", "expert"), None),
    )
    return jax.shard_map(
        on_device,
        mesh=mesh,
        in_specs=placed,
        out_specs=(P("dp", "expert"), P(None, ("dp", "expert"))),
        check_vma=False,
    )
```

profile of v0, /device:TPU:0, one launch (start us, length us, event | category | flops | bytes accessed | tf_op | source)
XLA Modules:
  0.0 458.0 jit_solution(3934987838661928534)
XLA Ops:
  7.2 0.8 copy.31
  7.9 0.1 reshape.73
  8.1 0.8 copy.29
  8.8 0.1 eq.36
  9.0 0.1 fusion.3
  9.1 0.2 select_reduce_fusion
  9.3 0.7 convert_element_type.96
  10.0 5.2 %all-to-all-start = ((bf16[8,1,48]{2,1,0:T(2,128)(2,1)}), bf16[8,1,48]{2,1,0:T(2,128)(2,1)S(1)}, u32[]{:S(2)}, u32[]{:S(2)}) async-start(bf16[8,1,48]{2,1,0:T(2,128)(2,1)} %convert_element_type.96), calls=%async_computation | async-start | bytes 8192 | tf_op jit(solution)/shard_map/all_to_all | solution.py:63
  15.2 0.1 convert_element_type.78
  15.3 0.1 copy.30
  15.4 0.7 multiply_add_fusion
  16.1 0.1 convert_reduce_fusion
  16.2 20.0 %all_gather.13 = bf16[64,6144]{1,0:T(8,128)(2,1)S(1)} all-gather(bf16[64,1536]{1,0:T(8,128)(2,1)} %param.8), channel_id=1, replica_groups=mesh['dp'=8,'expert'=4] {'expert'}, dimensions={1}, use_global_device_ids=true | all-gather | bytes 983040 | tf_op jit(solution)/shard_map/all_gather | solution.py:57
  36.2 3.6 convolution_convert_fusion
  39.7 0.0 all-to-all-done
  39.7 0.0 copy-start.1
  39.7 4.7 %all-to-all-start.2 = ((bf16[8,48,6144]{2,1,0:T(8,128)(2,1)}), bf16[8,48,6144]{2,1,0:T(8,128)(2,1)}, u32[]{:S(2)}, u32[]{:S(2)}) async-start(bf16[8,48,6144]{2,1,0:T(8,128)(2,1)} %bitcast.31), calls=%async_computation.2 | async-start | bytes 9437184 | tf_op jit(solution)/shard_map/all_to_all | solution.py:61
  44.5 0.0 copy-done.1
  44.5 18.2 %all_gather.12 = bf16[64,6144]{1,0:T(8,128)(2,1)S(1)} all-gather(bf16[64,1536]{1,0:T(8,128)(2,1)S(1)} %copy-done.1), channel_id=1, replica_groups=mesh['dp'=8,'expert'=4] {'expert'}, dimensions={1}, use_global_device_ids=true | all-gather | bytes 983040 | tf_op jit(solution)/shard_map/all_gather | solution.py:58
  62.7 3.6 convolution_convert_fusion.1
  66.3 32.9 %all-to-all-done.2 = bf16[8,48,6144]{2,1,0:T(8,128)(2,1)} async-done(((bf16[8,48,6144]{2,1,0:T(8,128)(2,1)}), bf16[8,48,6144]{2,1,0:T(8,128)(2,1)}, u32[]{:S(2)}, u32[]{:S(2)}) %all-to-all-start.2) | async-done | bytes 4718624 | tf_op jit(solution)/shard_map/all_to_all | solution.py:61
  99.2 4.6 %all-to-all-start.1 = ((bf16[8,48,6144]{2,1,0:T(8,128)(2,1)}), bf16[8,48,6144]{2,1,0:T(8,128)(2,1)}, u32[]{:S(2)}, u32[]{:S(2)}) async-start(bf16[8,48,6144]{2,1,0:T(8,128)(2,1)} %bitcast.30), calls=%async_computation.1 | async-start | bytes 9437184 | tf_op jit(solution)/shard_map/all_to_all | solution.py:62
  103.8 0.2 reduce-scatter.2.cloned.1.call-start
  104.1 0.1 reshape.74
  104.2 14.9 %fusion.10 = f32[384,2048]{1,0:T(8,128)S(1)} fusion(bf16[384,6144]{1,0:T(8,128)(2,1)} %bitcast.3, bf16[6144,2048]{1,0:T(8,128)(2,1)} %param.12), kind=kOutput, calls=%fused_computation.29 | convolution fusion | flops 9663676416 | bytes 33030144 | tf_op jit(solution)/shard_map/dot_general | solution.py:16
  119.1 39.5 %all-to-all-done.1 = bf16[8,48,6144]{2,1,0:T(8,128)(2,1)} async-done(((bf16[8,48,6144]{2,1,0:T(8,128)(2,1)}), bf16[8,48,6144]{2,1,0:T(8,128)(2,1)}, u32[]{:S(2)}, u32[]{:S(2)}) %all-to-all-start.1) | async-done | bytes 4718624 | tf_op jit(solution)/shard_map/all_to_all | solution.py:62
  158.6 17.2 %convolution_multiply_fusion = f32[384,2048]{1,0:T(8,128)} fusion(bf16[384,6144]{1,0:T(8,128)(2,1)} %bitcast.1, bf16[2048,6144]{1,0:T(8,128)(2,1)} %param.14, f32[384]{0:T(512)S(1)} %reshape.74), kind=kOutput, calls=%fused_computation.6 | convolution fusion | flops 9664462848 | bytes 33031680 | tf_op jit(solution)/shard_map/dot_general | solution.py:18
  175.8 17.9 %multiply_convert_fusion.1.clone.4 = bf16[384,2048]{1,0:T(8,128)(2,1)} fusion(f32[384,2048]{1,0:T(8,128)S(1)} %fusion.10, f32[384,2048]{1,0:T(8,128)} %convolution_multiply_fusion, bf16[384,6144]{1,0:T(8,128)(2,1)} %bitcast.3, bf16[6144,2048]{1,0:T(8,128)(2,1)} %param.13), kind=kOutput, calls=%fused_computation.4.clone.clone.clone.1 | convolution fusion | flops 9671540736 | bytes 37748736 | tf_op jit(solution)/shard_map/dot_general | solution.py:17
  193.6 17.4 %fusion = f32[384,6144]{1,0:T(8,128)} fusion(bf16[6144,2048]{1,0:T(8,128)(2,1)} %param.12, bf16[384,2048]{1,0:T(8,128)(2,1)} %multiply_convert_fusion.1.clone.4), kind=kOutput, calls=%fused_computation.7 | convolution fusion | flops 9663676416 | bytes 36175872 | tf_op jit(solution)/shard_map/dot_general | solution.py:23
  211.0 18.9 %add_convert_fusion = bf16[384,6144]{1,0:T(8,128)(2,1)} fusion(f32[384,6144]{1,0:T(8,128)} %fusion, bf16[6144,2048]{1,0:T(8,128)(2,1)} %param.13, f32[384,2048]{1,0:T(8,128)} %convolution_multiply_fusion, f32[384,2048]{1,0:T(8,128)S(1)} %fusion.10), kind=kOutput, calls=%fused_computation | convolution fusion | flops 9673113600 | bytes 45613056 | tf_op jit(solution)/shard_map/dot_general | solution.py:24
  229.9 59.2 %all_to_all.21 = bf16[8,48,6144]{2,1,0:T(8,128)(2,1)} all-to-all(bf16[8,48,6144]{2,1,0:T(8,128)(2,1)} %bitcast.32), channel_id=1, replica_groups=mesh['dp'=8,'expert'=4] {'dp'}, dimensions={0} | all-to-all | bytes 9437184 | tf_op jit(solution)/shard_map/all_to_all | solution.py:68
  289.0 0.0 reduce-scatter.2.cloned.1.call-update
  289.1 0.0 all-gather.2.cloned.1.call-start
  289.1 83.1 %reduce-scatter.2.cloned.1.call-done = bf16[8,48,1536]{2,1,0:T(8,128)(2,1)} async-done(((bf16[8,48,6144]{2,1,0:T(8,128)(2,1)}), bf16[8,48,1536]{2,1,0:T(8,128)(2,1)}) %reduce-scatter.2.cloned.1.call-update) | async-done | bytes 1179664 | tf_op jit(solution)/shard_map/reduce_scatter | solution.py:69
  372.3 1.6 convolution_convert_fusion.2
  373.9 0.0 copy-start
  373.9 19.3 %all_gather.14 = bf16[64,6144]{1,0:T(8,128)(2,1)} all-gather(bf16[64,1536]{1,0:T(8,128)(2,1)S(1)} %convolution_convert_fusion.2), channel_id=1, replica_groups=mesh['dp'=8,'expert'=4] {'expert'}, dimensions={1}, use_global_device_ids=true | all-gather | bytes 983040 | tf_op jit(solution)/shard_map/all_gather | solution.py:85
  393.2 0.0 all-gather.2.cloned.1.call-update
  393.2 45.5 %all-gather.2.cloned.1.call-done = bf16[512,6144]{1,0:T(8,128)(2,1)} async-done(((bf16[64,6144]{1,0:T(8,128)(2,1)}), bf16[512,6144]{1,0:T(8,128)(2,1)}) %all-gather.2.cloned.1.call-update) | async-done | bytes 6291472 | tf_op jit(solution)/shard_map/all_gather | solution.py:87
  438.7 12.5 %convolution_negate_fusion = f32[512,1024]{1,0:T(8,128)} fusion(bf16[512,6144]{1,0:T(8,128)(2,1)} %all-gather.2.cloned.1.call-done, bf16[1024,6144]{1,0:T(8,128)(2,1)} %param.15), kind=kOutput, calls=%fused_computation.9 | convolution fusion | flops 6442975232 | bytes 20971520 | tf_op jit(solution)/shard_map/dot_general | solution.py:86
  451.2 0.0 copy-done
  (3 shorter events, 0.0 us)
Async XLA Ops:
  10.0 29.8 %all-to-all-start = ((bf16[8,1,48]{2,1,0:T(2,128)(2,1)}), bf16[8,1,48]{2,1,0:T(2,128)(2,1)S(1)}, u32[]{:S(2)}, u32[]{:S(2)}) async-start(bf16[8,1,48]{2,1,0:T(2,128)(2,1)} %convert_element_type.96), calls=%async_computation | async-start | bytes 8192 | tf_op jit(solution)/shard_map/all_to_all | solution.py:63
  39.7 4.7 %copy-start.1 = (bf16[64,1536]{1,0:T(8,128)(2,1)S(1)}, bf16[64,1536]{1,0:T(8,128)(2,1)}, u32[]{:S(2)}) copy-start(bf16[64,1536]{1,0:T(8,128)(2,1)} %param.9) | copy-start | bytes 589828
  39.7 59.5 %all-to-all-start.2 = ((bf16[8,48,6144]{2,1,0:T(8,128)(2,1)}), bf16[8,48,6144]{2,1,0:T(8,128)(2,1)}, u32[]{:S(2)}, u32[]{:S(2)}) async-start(bf16[8,48,6144]{2,1,0:T(8,128)(2,1)} %bitcast.31), calls=%async_computation.2 | async-start | bytes 9437184 | tf_op jit(solution)/shard_map/all_to_all | solution.py:61
  99.2 59.4 %all-to-all-start.1 = ((bf16[8,48,6144]{2,1,0:T(8,128)(2,1)}), bf16[8,48,6144]{2,1,0:T(8,128)(2,1)}, u32[]{:S(2)}, u32[]{:S(2)}) async-start(bf16[8,48,6144]{2,1,0:T(8,128)(2,1)} %bitcast.30), calls=%async_computation.1 | async-start | bytes 9437184 | tf_op jit(solution)/shard_map/all_to_all | solution.py:62
  103.8 268.4 %reduce-scatter.2.cloned.1.call-start = ((), (), s32[]{:S(2)}) async-start(), calls=%async_computation.5 | async-start | bytes 5898240 | tf_op jit(solution)/shard_map/reduce_scatter | solution.py:69
  289.1 149.7 %all-gather.2.cloned.1.call-start = ((), (), s32[]{:S(2)}) async-start(), calls=%async_computation.6 | async-start | bytes 7077888 | tf_op jit(solution)/shard_map/all_gather | solution.py:87
  373.9 77.3 %copy-start = (bf16[64,1536]{1,0:T(8,128)(2,1)}, bf16[64,1536]{1,0:T(8,128)(2,1)S(1)}, u32[]{:S(2)}) copy-start(bf16[64,1536]{1,0:T(8,128)(2,1)S(1)} %convolution_convert_fusion.2) | copy-start | bytes 589828
Sparse Core Ops, SparseCore 0:
  289.2 83.0 reduce-scatter.1
  393.4 45.3 all-gather.1
where the time goes:
time: 459 us; the launch traced here: 458 us
  waiting for transfers between devices  201 us (44%)
  blocking collectives  117 us (25%)
  matrix products  108 us (24%)
  starting transfers between devices  14.8 us (3%)
  between operations  14.1 us (3%)
    reduce_scatter x1, waiting for transfers between devices, on_device(): lax.psum_scatter(came_back.astype(jnp.float32).astype(jnp.bfloat16), 'exp...  83.1 us
    all_to_all x1, blocking collectives, on_device(): lax.all_to_all(partial_rows, 'dp', split_axis=0, concat_axis=0, tiled=True)  59.2 us
    all_gather x1, waiting for transfers between devices, on_device(): lax.all_gather(whole_grad, 'dp', axis=0, tiled=True)  45.5 us
    all_to_all x1, waiting for transfers between devices, on_device(): lax.all_to_all(dispatch(whole_dy), 'dp', split_axis=0, concat_axis=0, til...  39.5 us
    all_to_all x1, waiting for transfers between devices, on_device(): lax.all_to_all(dispatch(whole_x), 'dp', split_axis=0, concat_axis=0, tile...  32.9 us
    all_gather x1, blocking collectives, on_device(): lax.all_gather(tokens, 'expert', axis=1, tiled=True)  20 us
    all_gather x1, blocking collectives, on_device(): whole_grad = lax.all_gather(input_grad, 'expert', axis=1, tiled=True)  19.3 us
    dot_general x1, matrix products, owner_work(): lax.dot_general(grad_up, w_up, contract, preferred_element_type=jnp.float32)  18.9 us
  transfers between devices with their start and end apart: 5, of which 4 were waited for; matrix products, arithmetic and copies ran while one was open for 5% of the time, Pallas kernels for 0%

commit v1 on v0

--- a/solution.py
+++ b/solution.py
@@ -1,33 +1,359 @@
+import functools
+
 import jax
 import jax.numpy as jnp
 from jax import lax
+from jax.experimental import pallas as pl
+from jax.experimental.pallas import tpu as pltpu
 from jax.sharding import PartitionSpec as P
 
 E = 8
 TOP = 2
 MOST = 48
-
-
-def owner_work(rows_x, rows_dy, gates, w_gate, w_up, w_down):
-    sources, slots, width = rows_x.shape
-    flat_x = rows_x.reshape(sources * slots, width)
-    flat_dy = rows_dy.reshape(sources * slots, width)
-    contract = (((1,), (1,)), ((), ()))
-    gate_pre = jnp.dot(flat_x, w_gate, preferred_element_type=jnp.float32)
-    up_pre = jnp.dot(flat_x, w_up, preferred_element_type=jnp.float32)
-    down_back = lax.dot_general(flat_dy, w_down, contract, preferred_element_type=jnp.float32)
-    scaled = gates.reshape(sources * slots, 1).astype(jnp.float32) * down_back
+MESH = pl.DeviceIdType.MESH
+HBM = pl.BlockSpec(memory_space=pl.ANY)
+VMEM = pl.BlockSpec(memory_space=pltpu.VMEM)
+GRANT = 60 * 1024 * 1024
+
+
+def places():
+    dp = lax.axis_index("dp")
+    z = lax.axis_index("expert")
+    core = lax.rem(dp, 2)
+    x = lax.rem(dp // 2, 2)
+    y = dp // 4
+    dx = 2 - 4 * x
+    dy = 4 - 8 * y
+    dc = 1 - 2 * core
+    return dp, z, dx, dy, dc
+
+
+def meet(dp, z, others):
+    barrier = pltpu.get_barrier_semaphore()
+    for d in others:
+        pl.semaphore_signal(barrier, inc=1, device_id=d, device_id_type=MESH)
+    pl.semaphore_wait(barrier, len(others))
+
+
+def gather_kernel(count, with_meta, *refs):
+    ins = refs[:count]
+    at = count
+    if with_meta:
+        meta_in = refs[at]
+        at += 1
+    outs = refs[at : at + count]
+    at += count
+    if with_meta:
+        meta_out = refs[at]
+        at += 1
+    send, recv, own, msend, mrecv = refs[at:]
+    dp, z, dx, dy, dc = places()
+    rows, cols = ins[0].shape
+    xn, yn, sib = dp + dx, dp + dy, dp + dc
+    dg = dp + dx + dy
+    zs = [lax.rem(z + d, 4) for d in range(4)]
+    dps = [lax.rem(dp + d, 8) for d in range(8)]
+    meet(dp, z, [(dp, zs[d]) for d in (1, 2, 3)] + [(dps[d], z) for d in range(1, 8)])
+
+    def block(a, src, q, lo=0, n=rows):
+        return outs[a].at[
+            pl.ds(pl.multiple_of(src * rows + lo, 16), n), pl.ds(pl.multiple_of(q * cols, 128), cols)
+        ]
+
+    def remote(src, dst, i, kind, dev):
+        return pltpu.make_async_remote_copy(
+            src_ref=src, dst_ref=dst, send_sem=send.at[i, kind], recv_sem=recv.at[i, kind],
+            device_id=dev, device_id_type=MESH,
+        )
+
+    sent = []
+
+    def go(c):
+        c.start()
+        sent.append(c)
+
+    local = []
+    if with_meta:
+        here = pl.ds(pl.multiple_of(dp * rows, 16), rows)
+        metas = []
+        for d in range(1, 8):
+            c = pltpu.make_async_remote_copy(
+                src_ref=meta_in, dst_ref=meta_out.at[here, :], send_sem=msend.at[d], recv_sem=mrecv.at[d],
+                device_id=(dps[d], z), device_id_type=MESH,
+            )
+            c.start()
+            metas.append(c)
+        c = pltpu.make_async_copy(meta_in, meta_out.at[here, :], own.at[count])
+        c.start()
+        local.append(c)
+    half = rows // 2
+    for a in range(count):
+        c = pltpu.make_async_copy(ins[a], block(a, dp, z), own.at[a])
+        c.start()
+        local.append(c)
+
+    def q_of(d):
+        return lax.rem(z + 4 - d, 4)
+
+    def stage0(i):
+        a, d = divmod(i, 4)
+        if d == 0:
+            for k in (1, 2, 3):
+                go(remote(ins[a], block(a, dp, z), a * 4 + k, 0, (dp, zs[k])))
+            src = ins[a]
+        else:
+            q = q_of(d)
+            remote(block(a, dp, q), block(a, dp, q), i, 0, (dp, z)).wait_recv()
+            src = block(a, dp, q)
+        q = q_of(d)
+        go(remote(src, block(a, dp, q), i, 1, (xn, z)))
+        go(remote(src, block(a, dp, q), i, 2, (yn, z)))
+        go(remote(src, block(a, dp, q), i, 5, (sib, z)))
+
+    def stage1(i):
+        a, d = divmod(i, 4)
+        q = q_of(d)
+        b = block(a, xn, q)
+        remote(b, b, i, 1, (xn, z)).wait_recv()
+        h = block(a, xn, q, 0, half)
+        go(remote(h, h, i, 3, (yn, z)))
+        go(remote(b, b, i, 6, (sib, z)))
+        b = block(a, yn, q)
+        remote(b, b, i, 2, (yn, z)).wait_recv()
+        h = block(a, yn, q, half, half)
+        go(remote(h, h, i, 4, (xn, z)))
+        go(remote(b, b, i, 7, (sib, z)))
+
+    def stage2(i):
+        a, d = divmod(i, 4)
+        q = q_of(d)
+        h = block(a, dg, q, 0, half)
+        remote(h, h, i, 3, (yn, z)).wait_recv()
+        h = block(a, dg, q, half, half)
+        remote(h, h, i, 4, (xn, z)).wait_recv()
+        b = block(a, dg, q)
+        go(remote(b, b, i, 8, (sib, z)))
+
+    total = 4 * count
+    for t in range(total + 2):
+        if t < total:
+            stage0(t)
+        if 0 <= t - 1 < total:
+            stage1(t - 1)
+        if 0 <= t - 2 < total:
+            stage2(t - 2)
+    for i in range(total):
+        a, d = divmod(i, 4)
+        q = q_of(d)
+        for k, src in ((5, sib), (6, xn + dc), (7, yn + dc), (8, dg + dc)):
+            b = block(a, src, q)
+            remote(b, b, i, k, (sib, z)).wait_recv()
+    if with_meta:
+        for d in range(1, 8):
+            metas[d - 1].wait()
+    for c in local:
+        c.wait()
+    for c in sent:
+        c.wait_send()
+
+
+def gather(arrays, meta, collective_id):
+    count = len(arrays)
+    rows, cols = arrays[0].shape
+    out = [jax.ShapeDtypeStruct((rows * 8, cols * 4), jnp.bfloat16)] * count
+    args = list(arrays)
+    if meta is not None:
+        args.append(meta)
+        out.append(jax.ShapeDtypeStruct((rows * 8, meta.shape[1]), jnp.bfloat16))
+    return pl.pallas_call(
+        functools.partial(gather_kernel, count, meta is not None),
+        out_shape=out,
+        in_specs=[VMEM] * len(args),
+        out_specs=[HBM] * len(out),
+        scratch_shapes=[
+            pltpu.SemaphoreType.DMA((4 * count, 9)),
+            pltpu.SemaphoreType.DMA((4 * count, 9)),
+            pltpu.SemaphoreType.DMA((count + 1,)),
+            pltpu.SemaphoreType.DMA((8,)),
+            pltpu.SemaphoreType.DMA((8,)),
+        ],
+        compiler_params=pltpu.CompilerParams(
+            collective_id=collective_id, has_side_effects=True, vmem_limit_bytes=GRANT
+        ),
+    )(*args)
+
+
+def reduce_kernel(p_ref, out_ref, got_s, got_d, got_x, got_y, got_z, acc, send, recv):
+    dp, z, dx, dy, dc = places()
+    rows, cols = out_ref.shape
+    half = rows // 2
+    xn, yn, sib, dg = dp + dx, dp + dy, dp + dc, dp + dx + dy
+    zs = [lax.rem(z + d, 4) for d in range(4)]
+    meet(dp, z, [(dp, zs[d]) for d in (1, 2, 3)] + [(xn, z), (yn, z), (sib, z)])
+    f32 = jnp.float32
+
+    def remote(src, dst, i, kind, dev):
+        return pltpu.make_async_remote_copy(
+            src_ref=src, dst_ref=dst, send_sem=send.at[i, kind], recv_sem=recv.at[i, kind],
+            device_id=dev, device_id_type=MESH,
+        )
+
+    sent = []
+
+    def go(c):
+        c.start()
+        sent.append(c)
+
+    lo, hi = pl.ds(0, half), pl.ds(half, half)
+    order = [zs[2], zs[1], zs[3], zs[0]]
+    slots = [(3, dg), (1, xn), (2, yn), (0, dp)]
+    for i in range(4):
+        q = order[i]
+        for s, owner in slots:
+            go(remote(p_ref.at[q, owner + dc], got_s.at[q, s], i, s, (sib, z)))
+
+    def arrive_s(i, s):
+        remote(got_s.at[order[i], s], got_s.at[order[i], s], i, s, (sib, z)).wait_recv()
+
+    def fold_diag(i):
+        q = order[i]
+        arrive_s(i, 3)
+        acc[q, 3] = (p_ref[q, dg].astype(f32) + got_s[q, 3].astype(f32)).astype(jnp.bfloat16)
+        go(remote(acc.at[q, 3, lo, :], got_d.at[q, 0], i, 4, (yn, z)))
+        go(remote(acc.at[q, 3, hi, :], got_d.at[q, 1], i, 5, (xn, z)))
+
+    def fold_side(i):
+        q = order[i]
+        arrive_s(i, 1)
+        remote(got_d.at[q, 0], got_d.at[q, 0], i, 4, (yn, z)).wait_recv()
+        acc[q, 1, lo, :] = (
+            p_ref[q, xn, lo, :].astype(f32) + got_s[q, 1, lo, :].astype(f32) + got_d[q, 0].astype(f32)
+        ).astype(jnp.bfloat16)
+        acc[q, 1, hi, :] = (
+            p_ref[q, xn, hi, :].astype(f32) + got_s[q, 1, hi, :].astype(f32)
+        ).astype(jnp.bfloat16)
+        go(remote(acc.at[q, 1], got_x.at[q], i, 6, (xn, z)))
+        arrive_s(i, 2)
+        remote(got_d.at[q, 1], got_d.at[q, 1], i, 5, (xn, z)).wait_recv()
+        acc[q, 2, hi, :] = (
+            p_ref[q, yn, hi, :].astype(f32) + got_s[q, 2, hi, :].astype(f32) + got_d[q, 1].astype(f32)
+        ).astype(jnp.bfloat16)
+        acc[q, 2, lo, :] = (
+            p_ref[q, yn, lo, :].astype(f32) + got_s[q, 2, lo, :].astype(f32)
+        ).astype(jnp.bfloat16)
+        go(remote(acc.at[q, 2], got_y.at[q], i, 7, (yn, z)))
+
+    def fold_own(i):
+        q = order[i]
+        arrive_s(i, 0)
+        remote(got_x.at[q], got_x.at[q], i, 6, (xn, z)).wait_recv()
+        remote(got_y.at[q], got_y.at[q], i, 7, (yn, z)).wait_recv()
+        total = (
+            p_ref[q, dp].astype(f32) + got_s[q, 0].astype(f32) + got_x[q].astype(f32) + got_y[q].astype(f32)
+        )
+        if i < 3:
+            acc[q, 0] = total.astype(jnp.bfloat16)
+            go(remote(acc.at[q, 0], got_z.at[i], i, 8, (dp, q)))
+            return None
+        for k in range(3):
+            remote(got_z.at[k], got_z.at[k], k, 8, (dp, z)).wait_recv()
+            total = total + got_z[k].astype(f32)
+        out_ref[...] = total.astype(jnp.bfloat16)
+
+    for t in range(6):
+        if t < 4:
+            fold_diag(t)
+        if 0 <= t - 1 < 4:
+            fold_side(t - 1)
+        if 0 <= t - 2 < 4:
+            fold_own(t - 2)
+    for c in sent:
+        c.wait_send()
+
+
+def reduce_scatter(dense, rows, cols, collective_id):
+    bf = jnp.bfloat16
+    return pl.pallas_call(
+        reduce_kernel,
+        out_shape=jax.ShapeDtypeStruct((rows, cols), bf),
+        in_specs=[VMEM],
+        out_specs=VMEM,
+        scratch_shapes=[
+            pltpu.VMEM((4, 4, rows, cols), bf),
+            pltpu.VMEM((4, 2, rows // 2, cols), bf),
+            pltpu.VMEM((4, rows, cols), bf),
+            pltpu.VMEM((4, rows, cols), bf),
+            pltpu.VMEM((3, rows, cols), bf),
+            pltpu.VMEM((4, 4, rows, cols), bf),
+            pltpu.SemaphoreType.DMA((4, 9)),
+            pltpu.SemaphoreType.DMA((4, 9)),
+        ],
+        compiler_params=pltpu.CompilerParams(
+            collective_id=collective_id, has_side_effects=True, vmem_limit_bytes=GRANT
+        ),
+    )(dense)
+
+
+CONTRACT = (((1,), (1,)), ((), ()))
+
+
+def expert_rows(flat_x, flat_dy, gates, w_gate, w_up, w_down):
+    f32 = jnp.float32
+    gate_pre = jnp.dot(flat_x, w_gate, preferred_element_type=f32)
+    up_pre = jnp.dot(flat_x, w_up, preferred_element_type=f32)
+    scaled = gates * lax.dot_general(flat_dy, w_down, CONTRACT, preferred_element_type=f32)
     sigma = jax.nn.sigmoid(gate_pre)
     grad_gate = (scaled * up_pre * sigma * (1.0 + gate_pre * (1.0 - sigma))).astype(jnp.bfloat16)
     grad_up = (scaled * gate_pre * sigma).astype(jnp.bfloat16)
-    partial_rows = lax.dot_general(grad_gate, w_gate, contract, preferred_element_type=jnp.float32)
-    partial_rows = partial_rows + lax.dot_general(
-        grad_up, w_up, contract, preferred_element_type=jnp.float32
-    )
-    return partial_rows.reshape(sources, slots, width)
-
-
-def on_device(tokens, cotangent, expert_ids, routing_weights, w_gate, w_up, w_down, embedding):
+    part = lax.dot_general(grad_gate, w_gate, CONTRACT, preferred_element_type=f32)
+    part = part + lax.dot_general(grad_up, w_up, CONTRACT, preferred_element_type=f32)
+    return part.astype(jnp.bfloat16)
+
+
+def on_device_block(tokens, cotangent, expert_ids, routing_weights, w_gate, w_up, w_down, embedding):
+    f32, bf = jnp.float32, jnp.bfloat16
+    rows, cols = tokens.shape
+    count = rows * 8
+    meta = jnp.concatenate(
+        [expert_ids.astype(bf), routing_weights, jnp.zeros((rows, 128 - 2 * TOP), bf)], axis=1
+    )
+    all_x, all_dy, all_meta = gather([tokens, cotangent], meta, 1)
+    mine = lax.axis_index("dp").astype(f32)
+    named = all_meta[:, :TOP].astype(f32) == mine
+    match = jnp.sum(named.astype(f32), axis=1)
+    weight = jnp.sum(jnp.where(named, all_meta[:, TOP : 2 * TOP].astype(f32), 0.0), axis=1)
+    row = jnp.arange(count, dtype=jnp.int32)
+    earlier = (row[None, :] < row[:, None]).astype(bf)
+    rank = jnp.dot(earlier, match.astype(bf)[:, None], preferred_element_type=f32)[:, 0].astype(jnp.int32)
+    slot = jnp.arange(E * MOST, dtype=jnp.int32)
+    chosen = (slot[:, None] == rank[None, :]) & (match[None, :] > 0.5)
+    select = chosen.astype(bf)
+    gates = jnp.sum(jnp.where(chosen, weight[None, :], 0.0), axis=1, keepdims=True)
+    flat_x = jnp.dot(select, all_x, preferred_element_type=f32).astype(bf)
+    flat_dy = jnp.dot(select, all_dy, preferred_element_type=f32).astype(bf)
+    part = expert_rows(flat_x, flat_dy, gates, w_gate, w_up, w_down)
+    dense = lax.dot_general(select, part, (((0,), (0,)), ((), ())), preferred_element_type=f32).astype(bf)
+    dense = dense.reshape(8, rows, 4, cols).transpose(2, 0, 1, 3)
+    input_grad = reduce_scatter(dense, rows, cols, 2)
+    (whole,) = gather([input_grad], None, 3)
+    scores = -lax.dot_general(whole, embedding, CONTRACT, preferred_element_type=f32)
+    return input_grad, scores
+
+
+def owner_work(rows_x, rows_dy, gates, w_gate, w_up, w_down):
+    sources, slots, width = rows_x.shape
+    part = expert_rows(
+        rows_x.reshape(sources * slots, width),
+        rows_dy.reshape(sources * slots, width),
+        gates.reshape(sources * slots, 1).astype(jnp.float32),
+        w_gate,
+        w_up,
+        w_down,
+    )
+    return part.reshape(sources, slots, width)
+
+
+def on_device_any(tokens, cotangent, expert_ids, routing_weights, w_gate, w_up, w_down, embedding):
     dp_count = lax.axis_size("dp")
     owners = dp_count // E
     tok_rows = tokens.shape[0]
@@ -62,9 +388,7 @@
         lax.all_to_all(dispatch(whole_dy), "dp", split_axis=0, concat_axis=0, tiled=True),
         lax.all_to_all(send_gates, "dp", split_axis=0, concat_axis=0, tiled=True),
     )
-    partial_rows = owner_work(recv_x, recv_dy, recv_gates, w_gate, w_up, w_down).astype(
-        jnp.bfloat16
-    )
+    partial_rows = owner_work(recv_x, recv_dy, recv_gates, w_gate, w_up, w_down)
     came_back = lax.all_to_all(partial_rows, "dp", split_axis=0, concat_axis=0, tiled=True)
     returned = lax.psum_scatter(
         came_back.astype(jnp.float32).astype(jnp.bfloat16),
@@ -103,8 +427,9 @@
         P(("dp", "expert"), None),
         P(("dp", "expert"), None),
     )
+    block = mesh.shape["dp"] == 8 and mesh.shape["expert"] == 4
     return jax.shard_map(
-        on_device,
+        on_device_block if block else on_device_any,
         mesh=mesh,
         in_specs=placed,
         out_specs=(P("dp", "expert"), P(None, ("dp", "expert"))),

time: 459 us -> 285 us (0.62)
  waiting for transfers between devices: 201 us -> 0 us
  Pallas kernels: 0 us -> 145 us
  blocking collectives: 117 us -> 0 us
  local copies, waits for them, and re-layouts: 2.78 us -> 23.6 us
  starting transfers between devices: 14.8 us -> 0 us
  between operations: 14.1 us -> 0.73 us
    pallas_call x0 -> x3, Pallas kernels: none -> 145 us  [the longest x2 106 us: gather(): pl.pallas_call(functools.partial(gather_kernel, count, meta is not None),...]
    reduce_scatter x1 -> x0, waiting for transfers between devices: 83.1 us -> none  [on_device(): lax.psum_scatter(came_back.astype(jnp.float32).astype(jnp.bfloat16), 'exp...]
    all_to_all x3 -> x0, waiting for transfers between devices: 72.4 us -> none  [the longest x1 39.5 us: on_device(): lax.all_to_all(dispatch(whole_dy), 'dp', split_axis=0, concat_axis=0, til...]
    all_to_all x1 -> x0, blocking collectives: 59.2 us -> none  [on_device(): lax.all_to_all(partial_rows, 'dp', split_axis=0, concat_axis=0, tiled=True)]
    all_gather x3 -> x0, blocking collectives: 57.5 us -> none  [the longest x1 20 us: on_device(): lax.all_gather(tokens, 'expert', axis=1, tiled=True)]
    all_gather x1 -> x0, waiting for transfers between devices: 45.5 us -> none  [on_device(): lax.all_gather(whole_grad, 'dp', axis=0, tiled=True)]
    reshape x0 -> x2, local copies, waits for them, and re-layouts: none -> 20.3 us  [on_device_block(): dense = dense.reshape(8, rows, 4, cols).transpose(2, 0, 1, 3)]
    all_to_all x3 -> x0, starting transfers between devices: 14.5 us -> none  [the longest x1 5.17 us: on_device(): lax.all_to_all(send_gates, 'dp', split_axis=0, concat_axis=0, tiled=True)]
  transfers between devices with their start and end apart: 5 -> 0, of which waited for: 4 -> 0; matrix products, arithmetic and copies ran while one was open for 5% -> 0% of each run, Pallas kernels for 0% -> 0%
where the time goes in v1:
time: 285 us; the launch traced here: 284 us
  Pallas kernels  145 us (51%)
  matrix products  112 us (39%)
  local copies, waits for them, and re-layouts  23.6 us (8%)
  other arithmetic  2.87 us (1%)
    pallas_call x2, Pallas kernels, gather(): pl.pallas_call(functools.partial(gather_kernel, count, meta is not None),...  106 us
    pallas_call x1, Pallas kernels, reduce_scatter(): pl.pallas_call(reduce_kernel, out_shape=jax.ShapeDtypeStruct((rows, cols)...  39.2 us
    reshape x2, local copies, waits for them, and re-layouts, on_device_block(): dense = dense.reshape(8, rows, 4, cols).transpose(2, 0, 1, 3)  20.3 us
    dot_general x1, matrix products, expert_rows(): lax.dot_general(grad_up, w_up, CONTRACT, preferred_element_type=f32)  18.8 us
    dot_general x1, matrix products, expert_rows(): lax.dot_general(grad_gate, w_gate, CONTRACT, preferred_element_type=f32)  17.3 us
    dot_general x1, matrix products, expert_rows(): lax.dot_general(flat_dy, w_down, CONTRACT, preferred_element_type=f32)  17.1 us
    dot_general x1, matrix products, expert_rows(): up_pre = jnp.dot(flat_x, w_up, preferred_element_type=f32)  16.1 us
    dot_general x1, matrix products, expert_rows(): gate_pre = jnp.dot(flat_x, w_gate, preferred_element_type=f32)  15 us

profile of v1, /device:TPU:0, one launch (start us, length us, event | category | flops | bytes accessed | tf_op | source)
XLA Modules:
  0.0 284.0 jit_solution(15089886210886572664)
XLA Ops:
  0.6 0.7 convert_element_type.45
  1.3 0.1 pad.2.clone
  1.4 0.1 copy.15
  1.5 0.8 copy.16
  2.3 0.7 maximum_maximum_fusion.refs_2_
  3.0 67.8 %shard_map.95 = (bf16[512,6144]{1,0:T(8,128)(2,1)}, bf16[512,6144]{1,0:T(8,128)(2,1)}, bf16[512,128]{1,0:T(8,128)(2,1)}) custom-call(bf16[64,1536]{1,0:T(8,128)(2,1)} %refs_0_.1, bf16[64,1536]{1,0:T(8,128)(2,1)} %refs_1_.1, bf16[64,128]{1,0:T(8,128)(2,1)} %maximum_maximum_fusion.refs_2_), custom_call_target="tpu_custom_call" | custom-call | tf_op jit(solution)/shard_map/pallas_call | solution.py:168
  70.8 1.2 select_reduce_fusion.1
  72.1 0.2 fusion.3
  72.3 7.0 %convolution_convert_fusion.1 = bf16[384,6144]{1,0:T(8,128)(2,1)} fusion(bf16[512,6144]{1,0:T(8,128)(2,1)} %get-tuple-element.7, s32[512]{0:T(512)S(1)} %convert_element_type.50, pred[512]{0:T(512)(128)(4,1)S(1)} %broadcast_compare_fusion), kind=kOutput, calls=%fused_computation.2 | convolution fusion | flops 2418671616 | bytes 11012608 | tf_op jit(solution)/shard_map/dot_general | solution.py:332
  79.3 0.2 select_reduce_fusion
  79.6 17.1 %convolution_multiply_fusion = f32[384,2048]{1,0:T(8,128)S(1)} fusion(bf16[2048,6144]{1,0:T(8,128)(2,1)} %param.14, f32[384]{0:T(512)S(1)} %select_reduce_fusion, bf16[512,6144]{1,0:T(8,128)(2,1)} %get-tuple-element.6, s32[512]{0:T(512)S(1)} %convert_element_type.50, pred[512]{0:T(512)(128)(4,1)S(1)} %broadcast_compare_fusion), kind=kOutput, calls=%fused_computation.8 | convolution fusion | flops 12083134464 | bytes 34607104 | tf_op jit(solution)/shard_map/dot_general | solution.py:304
  96.7 0.0 copy-start.1
  96.7 15.0 %fusion.19 = f32[384,2048]{1,0:T(8,128)S(1)} fusion(bf16[384,6144]{1,0:T(8,128)(2,1)} %convolution_convert_fusion.1, bf16[6144,2048]{1,0:T(8,128)(2,1)} %param.12), kind=kOutput, calls=%fused_computation.31 | convolution fusion | flops 9663676416 | bytes 33030144 | tf_op jit(solution)/shard_map/dot_general | solution.py:302
  111.7 0.0 copy-start.2
  111.7 1.7 copy-done.2
  113.4 0.0 copy-done.1
  113.4 16.1 %multiply_convert_fusion.1.clone.4 = bf16[384,2048]{1,0:T(8,128)(2,1)} fusion(f32[384,2048]{1,0:T(8,128)S(1)} %fusion.19, f32[384,2048]{1,0:T(8,128)S(1)} %convolution_multiply_fusion, bf16[384,6144]{1,0:T(8,128)(2,1)S(1)} %copy-done.1, bf16[6144,2048]{1,0:T(8,128)(2,1)} %param.13), kind=kOutput, calls=%fused_computation.6.clone.clone.clone.1 | convolution fusion | flops 9671540736 | bytes 37748736 | tf_op jit(solution)/shard_map/dot_general | solution.py:303
  129.5 17.3 %fusion = f32[384,6144]{1,0:T(8,128)} fusion(bf16[6144,2048]{1,0:T(8,128)(2,1)} %param.12, bf16[384,2048]{1,0:T(8,128)(2,1)} %multiply_convert_fusion.1.clone.4), kind=kOutput, calls=%fused_computation.9 | convolution fusion | flops 9663676416 | bytes 36175872 | tf_op jit(solution)/shard_map/dot_general | solution.py:308
  146.7 18.8 %add_convert_fusion = bf16[384,6144]{1,0:T(8,128)(2,1)} fusion(f32[384,6144]{1,0:T(8,128)} %fusion, bf16[6144,2048]{1,0:T(8,128)(2,1)} %param.13, f32[384,2048]{1,0:T(8,128)S(1)} %convolution_multiply_fusion, f32[384,2048]{1,0:T(8,128)} %copy-done.2), kind=kOutput, calls=%fused_computation | convolution fusion | flops 9673113600 | bytes 45613056 | tf_op jit(solution)/shard_map/dot_general | solution.py:309
  165.5 7.8 %convolution_convert_fusion = bf16[512,6144]{1,0:T(8,128)(2,1)} fusion(bf16[384,6144]{1,0:T(8,128)(2,1)} %add_convert_fusion, s32[512]{0:T(512)S(1)} %convert_element_type.50, pred[512]{0:T(512)(128)(4,1)S(1)} %broadcast_compare_fusion), kind=kOutput, calls=%fused_computation.1 | convolution fusion | flops 2419458048 | bytes 11012608 | tf_op jit(solution)/shard_map/dot_general | solution.py:335
  173.3 13.4 %reshape.20 = bf16[8,64,4,1536]{3,2,1,0:T(4,128)(2,1)} reshape(bf16[512,6144]{1,0:T(8,128)(2,1)} %convolution_convert_fusion) | data formatting | bytes 12582912 | tf_op jit(solution)/shard_map/reshape | solution.py:336
  186.7 6.9 %copy.19 = bf16[8,64,4,1536]{3,1,0,2:T(8,128)(2,1)} copy(bf16[8,64,4,1536]{3,2,1,0:T(4,128)(2,1)} %reshape.20) | data formatting | bytes 12582912 | tf_op jit(solution)/shard_map/reshape | solution.py:336
  193.6 39.2 %shard_map.96.refs_0_ = bf16[64,1536]{1,0:T(8,128)(2,1)} custom-call(bf16[4,8,64,1536]{3,2,1,0:T(8,128)(2,1)} %bitcast.25), custom_call_target="tpu_custom_call" | custom-call | tf_op jit(solution)/shard_map/pallas_call | solution.py:276
  232.8 38.0 %shard_map.97 = bf16[512,6144]{1,0:T(8,128)(2,1)} custom-call(bf16[64,1536]{1,0:T(8,128)(2,1)} %shard_map.96.refs_0_), custom_call_target="tpu_custom_call" | custom-call | tf_op jit(solution)/shard_map/pallas_call | solution.py:168
  270.8 0.0 copy-start
  270.8 12.5 %convolution_negate_fusion = f32[512,1024]{1,0:T(8,128)} fusion(bf16[512,6144]{1,0:T(8,128)(2,1)} %shard_map.97, bf16[1024,6144]{1,0:T(8,128)(2,1)} %param.15), kind=kOutput, calls=%fused_computation.10 | convolution fusion | flops 6442975232 | bytes 20971520 | tf_op jit(solution)/shard_map/dot_general | solution.py:339
  283.3 0.0 copy-done
  283.3 0.7 copy.21
  (5 shorter events, 0.0 us)
Async XLA Ops:
  96.7 16.7 %copy-start.1 = (bf16[384,6144]{1,0:T(8,128)(2,1)S(1)}, bf16[384,6144]{1,0:T(8,128)(2,1)}, u32[]{:S(2)}) copy-start(bf16[384,6144]{1,0:T(8,128)(2,1)} %convolution_convert_fusion.1) | copy-start | bytes 14155780
  111.7 1.7 copy-start.2
  270.8 12.5 %copy-start = (bf16[64,1536]{1,0:T(8,128)(2,1)S(1)}, bf16[64,1536]{1,0:T(8,128)(2,1)}, u32[]{:S(2)}) copy-start(bf16[64,1536]{1,0:T(8,128)(2,1)} %shard_map.96.refs_0_) | copy-start | bytes 589828

commit v2 on v1

--- a/solution.py
+++ b/solution.py
@@ -192,6 +192,14 @@
     meet(dp, z, [(dp, zs[d]) for d in (1, 2, 3)] + [(xn, z), (yn, z), (sib, z)])
     f32 = jnp.float32
 
+    def p_at(q, owner, lo=0, n=rows):
+        return p_ref.at[
+            pl.ds(pl.multiple_of(owner * rows + lo, 16), n), pl.ds(pl.multiple_of(q * cols, 128), cols)
+        ]
+
+    def mine(q, owner, lo=0, n=rows):
+        return p_at(q, owner, lo, n)[...].astype(f32)
+
     def remote(src, dst, i, kind, dev):
         return pltpu.make_async_remote_copy(
             src_ref=src, dst_ref=dst, send_sem=send.at[i, kind], recv_sem=recv.at[i, kind],
@@ -210,7 +218,7 @@
     for i in range(4):
         q = order[i]
         for s, owner in slots:
-            go(remote(p_ref.at[q, owner + dc], got_s.at[q, s], i, s, (sib, z)))
+            go(remote(p_at(q, owner + dc), got_s.at[q, s], i, s, (sib, z)))
 
     def arrive_s(i, s):
         remote(got_s.at[order[i], s], got_s.at[order[i], s], i, s, (sib, z)).wait_recv()
@@ -218,7 +226,7 @@
     def fold_diag(i):
         q = order[i]
         arrive_s(i, 3)
-        acc[q, 3] = (p_ref[q, dg].astype(f32) + got_s[q, 3].astype(f32)).astype(jnp.bfloat16)
+        acc[q, 3] = (mine(q, dg) + got_s[q, 3].astype(f32)).astype(jnp.bfloat16)
         go(remote(acc.at[q, 3, lo, :], got_d.at[q, 0], i, 4, (yn, z)))
         go(remote(acc.at[q, 3, hi, :], got_d.at[q, 1], i, 5, (xn, z)))
 
@@ -227,19 +235,19 @@
         arrive_s(i, 1)
         remote(got_d.at[q, 0], got_d.at[q, 0], i, 4, (yn, z)).wait_recv()
         acc[q, 1, lo, :] = (
-            p_ref[q, xn, lo, :].astype(f32) + got_s[q, 1, lo, :].astype(f32) + got_d[q, 0].astype(f32)
+            mine(q, xn, 0, half) + got_s[q, 1, lo, :].astype(f32) + got_d[q, 0].astype(f32)
         ).astype(jnp.bfloat16)
         acc[q, 1, hi, :] = (
-            p_ref[q, xn, hi, :].astype(f32) + got_s[q, 1, hi, :].astype(f32)
+            mine(q, xn, half, half) + got_s[q, 1, hi, :].astype(f32)
         ).astype(jnp.bfloat16)
         go(remote(acc.at[q, 1], got_x.at[q], i, 6, (xn, z)))
         arrive_s(i, 2)
         remote(got_d.at[q, 1], got_d.at[q, 1], i, 5, (xn, z)).wait_recv()
         acc[q, 2, hi, :] = (
-            p_ref[q, yn, hi, :].astype(f32) + got_s[q, 2, hi, :].astype(f32) + got_d[q, 1].astype(f32)
+            mine(q, yn, half, half) + got_s[q, 2, hi, :].astype(f32) + got_d[q, 1].astype(f32)
         ).astype(jnp.bfloat16)
         acc[q, 2, lo, :] = (
-            p_ref[q, yn, lo, :].astype(f32) + got_s[q, 2, lo, :].astype(f32)
+            mine(q, yn, 0, half) + got_s[q, 2, lo, :].astype(f32)
         ).astype(jnp.bfloat16)
         go(remote(acc.at[q, 2], got_y.at[q], i, 7, (yn, z)))
 
@@ -249,7 +257,7 @@
         remote(got_x.at[q], got_x.at[q], i, 6, (xn, z)).wait_recv()
         remote(got_y.at[q], got_y.at[q], i, 7, (yn, z)).wait_recv()
         total = (
-            p_ref[q, dp].astype(f32) + got_s[q, 0].astype(f32) + got_x[q].astype(f32) + got_y[q].astype(f32)
+            mine(q, dp) + got_s[q, 0].astype(f32) + got_x[q].astype(f32) + got_y[q].astype(f32)
         )
         if i < 3:
             acc[q, 0] = total.astype(jnp.bfloat16)
@@ -333,7 +341,6 @@
     flat_dy = jnp.dot(select, all_dy, preferred_element_type=f32).astype(bf)
     part = expert_rows(flat_x, flat_dy, gates, w_gate, w_up, w_down)
     dense = lax.dot_general(select, part, (((0,), (0,)), ((), ())), preferred_element_type=f32).astype(bf)
-    dense = dense.reshape(8, rows, 4, cols).transpose(2, 0, 1, 3)
     input_grad = reduce_scatter(dense, rows, cols, 2)
     (whole,) = gather([input_grad], None, 3)
     scores = -lax.dot_general(whole, embedding, CONTRACT, preferred_element_type=f32)

time: 285 us -> 265 us (0.930)
  local copies, waits for them, and re-layouts: 23.6 us -> 3.3 us
    reshape x2 -> x0, local copies, waits for them, and re-layouts: 20.3 us -> none  [on_device_block(): dense = dense.reshape(8, rows, 4, cols).transpose(2, 0, 1, 3)]
where the time goes in v2:
time: 265 us; the launch traced here: 264 us
  Pallas kernels  145 us (55%)
  matrix products  112 us (42%)
  local copies, waits for them, and re-layouts  3.3 us (1%)
  other arithmetic  2.87 us (1%)
    pallas_call x2, Pallas kernels, gather(): pl.pallas_call(functools.partial(gather_kernel, count, meta is not None),...  106 us
    pallas_call x1, Pallas kernels, reduce_scatter(): pl.pallas_call(reduce_kernel, out_shape=jax.ShapeDtypeStruct((rows, cols)...  39.2 us
    dot_general x1, matrix products, expert_rows(): lax.dot_general(grad_up, w_up, CONTRACT, preferred_element_type=f32)  18.7 us
    dot_general x1, matrix products, expert_rows(): lax.dot_general(grad_gate, w_gate, CONTRACT, preferred_element_type=f32)  17.3 us
    dot_general x1, matrix products, expert_rows(): lax.dot_general(flat_dy, w_down, CONTRACT, preferred_element_type=f32)  17.1 us
    dot_general x1, matrix products, expert_rows(): up_pre = jnp.dot(flat_x, w_up, preferred_element_type=f32)  16.3 us
    dot_general x1, matrix products, expert_rows(): gate_pre = jnp.dot(flat_x, w_gate, preferred_element_type=f32)  15 us
    dot_general x1, matrix products, on_device_block(): lax.dot_general(whole, embedding, CONTRACT, preferred_element_type=f32)  12.7 us

profile of v2, /device:TPU:0, one launch (start us, length us, event | category | flops | bytes accessed | tf_op | source)
XLA Modules:
  0.0 264.1 jit_solution(9570730392212833139)
XLA Ops:
  0.6 0.7 convert_element_type.45
  1.3 0.1 pad.2.clone
  1.4 0.1 copy.12
  1.5 0.8 copy.13
  2.3 0.7 maximum_maximum_fusion.refs_2_
  3.0 67.8 %shard_map.95 = (bf16[512,6144]{1,0:T(8,128)(2,1)}, bf16[512,6144]{1,0:T(8,128)(2,1)}, bf16[512,128]{1,0:T(8,128)(2,1)}) custom-call(bf16[64,1536]{1,0:T(8,128)(2,1)} %refs_0_.1, bf16[64,1536]{1,0:T(8,128)(2,1)} %refs_1_.1, bf16[64,128]{1,0:T(8,128)(2,1)} %maximum_maximum_fusion.refs_2_), custom_call_target="tpu_custom_call" | custom-call | tf_op jit(solution)/shard_map/pallas_call | solution.py:168
  70.8 1.2 select_reduce_fusion.1
  72.1 0.2 fusion.3
  72.3 7.0 %convolution_convert_fusion.1 = bf16[384,6144]{1,0:T(8,128)(2,1)} fusion(bf16[512,6144]{1,0:T(8,128)(2,1)} %get-tuple-element.7, s32[512]{0:T(512)S(1)} %convert_element_type.50, pred[512]{0:T(512)(128)(4,1)S(1)} %broadcast_compare_fusion), kind=kOutput, calls=%fused_computation.2 | convolution fusion | flops 2418671616 | bytes 11012608 | tf_op jit(solution)/shard_map/dot_general | solution.py:340
  79.3 0.2 select_reduce_fusion
  79.6 17.1 %convolution_multiply_fusion = f32[384,2048]{1,0:T(8,128)S(1)} fusion(bf16[2048,6144]{1,0:T(8,128)(2,1)} %param.14, f32[384]{0:T(512)S(1)} %select_reduce_fusion, bf16[512,6144]{1,0:T(8,128)(2,1)} %get-tuple-element.6, s32[512]{0:T(512)S(1)} %convert_element_type.50, pred[512]{0:T(512)(128)(4,1)S(1)} %broadcast_compare_fusion), kind=kOutput, calls=%fused_computation.7 | convolution fusion | flops 12083134464 | bytes 34607104 | tf_op jit(solution)/shard_map/dot_general | solution.py:312
  96.7 0.0 copy-start.1
  96.7 15.0 %fusion.19 = f32[384,2048]{1,0:T(8,128)S(1)} fusion(bf16[384,6144]{1,0:T(8,128)(2,1)} %convolution_convert_fusion.1, bf16[6144,2048]{1,0:T(8,128)(2,1)} %param.12), kind=kOutput, calls=%fused_computation.30 | convolution fusion | flops 9663676416 | bytes 33030144 | tf_op jit(solution)/shard_map/dot_general | solution.py:310
  111.7 0.0 copy-start.2
  111.7 1.7 copy-done.2
  113.4 0.0 copy-done.1
  113.4 16.3 %multiply_convert_fusion.1.clone.4 = bf16[384,2048]{1,0:T(8,128)(2,1)} fusion(f32[384,2048]{1,0:T(8,128)S(1)} %fusion.19, f32[384,2048]{1,0:T(8,128)S(1)} %convolution_multiply_fusion, bf16[384,6144]{1,0:T(8,128)(2,1)S(1)} %copy-done.1, bf16[6144,2048]{1,0:T(8,128)(2,1)} %param.13), kind=kOutput, calls=%fused_computation.5.clone.clone.clone.1 | convolution fusion | flops 9671540736 | bytes 37748736 | tf_op jit(solution)/shard_map/dot_general | solution.py:311
  129.7 17.3 %fusion = f32[384,6144]{1,0:T(8,128)} fusion(bf16[6144,2048]{1,0:T(8,128)(2,1)} %param.12, bf16[384,2048]{1,0:T(8,128)(2,1)} %multiply_convert_fusion.1.clone.4), kind=kOutput, calls=%fused_computation.8 | convolution fusion | flops 9663676416 | bytes 36175872 | tf_op jit(solution)/shard_map/dot_general | solution.py:316
  147.0 18.7 %add_convert_fusion = bf16[384,6144]{1,0:T(8,128)(2,1)} fusion(f32[384,6144]{1,0:T(8,128)} %fusion, bf16[6144,2048]{1,0:T(8,128)(2,1)} %param.13, f32[384,2048]{1,0:T(8,128)S(1)} %convolution_multiply_fusion, f32[384,2048]{1,0:T(8,128)} %copy-done.2), kind=kOutput, calls=%fused_computation | convolution fusion | flops 9673113600 | bytes 45613056 | tf_op jit(solution)/shard_map/dot_general | solution.py:317
  165.7 7.8 %convolution_convert_fusion.p_ref = bf16[512,6144]{1,0:T(8,128)(2,1)} fusion(bf16[384,6144]{1,0:T(8,128)(2,1)} %add_convert_fusion, s32[512]{0:T(512)S(1)} %convert_element_type.50, pred[512]{0:T(512)(128)(4,1)S(1)} %broadcast_compare_fusion), kind=kOutput, calls=%fused_computation.1 | convolution fusion | flops 2419458048 | bytes 11012608 | tf_op jit(solution)/shard_map/dot_general | solution.py:343
  173.5 39.2 %shard_map.96.refs_0_ = bf16[64,1536]{1,0:T(8,128)(2,1)} custom-call(bf16[512,6144]{1,0:T(8,128)(2,1)} %convolution_convert_fusion.p_ref), custom_call_target="tpu_custom_call" | custom-call | tf_op jit(solution)/shard_map/pallas_call | solution.py:284
  212.7 38.0 %shard_map.97 = bf16[512,6144]{1,0:T(8,128)(2,1)} custom-call(bf16[64,1536]{1,0:T(8,128)(2,1)} %shard_map.96.refs_0_), custom_call_target="tpu_custom_call" | custom-call | tf_op jit(solution)/shard_map/pallas_call | solution.py:168
  250.7 0.0 copy-start
  250.7 12.7 %convolution_negate_fusion = f32[512,1024]{1,0:T(8,128)} fusion(bf16[512,6144]{1,0:T(8,128)(2,1)} %shard_map.97, bf16[1024,6144]{1,0:T(8,128)(2,1)} %param.15), kind=kOutput, calls=%fused_computation.9 | convolution fusion | flops 6442975232 | bytes 20971520 | tf_op jit(solution)/shard_map/dot_general | solution.py:346
  263.4 0.0 copy-done
  263.4 0.7 copy.15
  (5 shorter events, 0.0 us)
Async XLA Ops:
  96.7 16.7 %copy-start.1 = (bf16[384,6144]{1,0:T(8,128)(2,1)S(1)}, bf16[384,6144]{1,0:T(8,128)(2,1)}, u32[]{:S(2)}) copy-start(bf16[384,6144]{1,0:T(8,128)(2,1)} %convolution_convert_fusion.1) | copy-start | bytes 14155780
  111.7 1.7 copy-start.2
  250.7 12.7 %copy-start = (bf16[64,1536]{1,0:T(8,128)(2,1)S(1)}, bf16[64,1536]{1,0:T(8,128)(2,1)}, u32[]{:S(2)}) copy-start(bf16[64,1536]{1,0:T(8,128)(2,1)} %shard_map.96.refs_0_) | copy-start | bytes 589828
